TPU v7x, 32 devices: a whole 2x2x4 slice. The times are simulated.
32 devices in a mesh: row: 4 (over y, core), col: 8 (over z, x).
Axes of the slice: x: 2, y: 2, z: 4, core: 2. Of those that a mesh axis runs over, the one named last changes fastest.
Arguments:
- factor: float32 [6, 2048, 6, 2048], P(None, 'row', None, 'col'), may hold values from -0.0625 to 0.0625
- diag_inv: float32 [6, 2048, 2048], P(None, None, 'row'), may hold values from -2 to 2, as said below
- structure: int32 [6, 6, 16], P(None, None, 'row'), may hold values 0 or 1
- parent: int32 [6], replicated, may hold values from 1 to 6, as said below
- post: float32 [6, 2048, 64], P(None, 'row', 'col'), may hold values from -6 to 6
Outputs:
- mean_x: float32 [6, 2048, 64], P(None, 'row', 'col')
- variance: float32 [6, 2048], P(None, 'row')
Inputs may be any that keep to these rules, and one draw needn't show every extreme that they name: parent[s] > s for s < 5, and parent[5] = 6; every supernode has at most 2 ancestors, and some supernode has exactly that many. The diagonal of each diag_inv[s] lies in 0.5 to 2.
All inputs are finite; a program needn't handle non-finite values. No bound on the sum of `structure` on one device may be relied on, other than what follows from the above.
Results may differ from a plain program's by a relative error of at most 0.00014.
Values sent between devices are 32-bit elements; how exact they have to be, the bound alone decides.
A program may use at most 192 MiB of HBM per device.

v0:
```python
import jax
import jax.numpy as jnp
from jax import lax
from jax.sharding import PartitionSpec as P

LEVELS = 3
HIGHEST = lax.Precision.HIGHEST


def contract(selected, panel_piece):
    return jnp.einsum("tiw,tin->wn", panel_piece, selected, precision=HIGHEST)


def body(factor, diag_inv, structure, parent, post):
    super_count = factor.shape[0]
    row_width = factor.shape[1]
    col_width = factor.shape[3]
    full_width = diag_inv.shape[1]
    rhs_width = post.shape[2]
    row_at = lax.axis_index("row")
    col_at = lax.axis_index("col")
    extended = jnp.concatenate([parent, jnp.full((1,), super_count, jnp.int32)])
    slot_ids = jnp.arange(super_count + 1, dtype=jnp.int32)
    targets = jnp.arange(super_count, dtype=jnp.int32)
    ancestor_hops = []
    current = parent
    for hop_index in range(super_count - 1):
        ancestor_hops.append(current)
        onehot = (current[:, None] == slot_ids[None, :]).astype(jnp.int32)
        current = jnp.sum(onehot * extended[None, :], axis=1)
    ancestry = jnp.zeros((super_count, super_count), jnp.float32)
    for hop_targets in ancestor_hops:
        ancestry = ancestry + (hop_targets[:, None] == targets[None, :]).astype(jnp.float32)
    block_rows = row_width // structure.shape[2]
    row_mask = jnp.repeat(structure.astype(jnp.float32), block_rows, axis=2) * ancestry[:, :, None]
    masked = factor * jnp.transpose(row_mask, (1, 2, 0))[:, :, :, None]
    rows_full = jnp.arange(full_width, dtype=jnp.int32)
    own_cols = row_at * row_width + jnp.arange(row_width, dtype=jnp.int32)
    lower_inv = jnp.where((rows_full[:, None] >= own_cols[None, :])[None, :, :], diag_inv, 0.0)
    unit_cols = col_at * col_width + jnp.arange(col_width, dtype=jnp.int32)
    unit_block = (rows_full[:, None] == unit_cols[None, :]).astype(jnp.float32)
    gathered = lax.all_gather(post, "row", axis=1, tiled=True)
    total_cols = super_count * col_width + rhs_width
    solution = jnp.zeros((super_count, row_width, total_cols), jnp.float32)
    for current_sup in range(super_count - 1, -1, -1):
        later_cols = (current_sup + 1) * col_width
        if current_sup == super_count - 1:
            summed = jnp.zeros((full_width, rhs_width), jnp.float32)
        else:
            picks = []
            chosen_rows = []
            for slot_index in range(LEVELS - 1):
                target = ancestor_hops[slot_index][current_sup]
                is_valid = (target < super_count).astype(jnp.float32)
                clamped = jnp.minimum(target, super_count - 1)
                picks.append(
                    lax.dynamic_index_in_dim(
                        masked[:, :, current_sup, :], clamped, 0, keepdims=False
                    )
                    * is_valid
                )
                chosen_rows.append(
                    lax.dynamic_index_in_dim(solution, clamped, 0, keepdims=False)[:, later_cols:]
                )
            blocks = jnp.stack(picks)
            selected = jnp.stack(chosen_rows)
            partial_value = contract(selected, lax.all_gather(blocks, "col", axis=2, tiled=True))
            summed = lax.psum(partial_value, "row")
        split_at = summed.shape[1] - rhs_width
        remaining = jnp.concatenate(
            [-summed[:, :split_at], gathered[current_sup] - summed[:, split_at:]], axis=1
        )
        right = jnp.concatenate([unit_block, remaining], axis=1)
        fresh = jnp.dot(
            lower_inv[current_sup].T, right, precision=HIGHEST, preferred_element_type=jnp.float32
        )
        solution = solution.at[current_sup, :, current_sup * col_width :].set(fresh)
    mean_x = solution[:, :, super_count * col_width :]
    unit_part = solution[:, :, : super_count * col_width]
    squares = jnp.sum(unit_part * unit_part, axis=2)
    variance = lax.psum(squares, "col")
    return (mean_x, variance)


def solution(mesh):
    return jax.shard_map(
        body,
        mesh=mesh,
        in_specs=(
            P(None, "row", None, "col"),
            P(None, None, "row"),
            P(None, None, "row"),
            P(),
            P(None, "row", "col"),
        ),
        out_specs=(P(None, "row", "col"), P(None, "row")),
        check_vma=False,
    )
```

profile of v0, /device:TPU:0, one launch (start us, length us, event | category | flops | bytes accessed | tf_op | source)
XLA Modules:
  0.0 1485.7 jit_solution(14807575500122001028)
XLA Ops:
  7.9 0.8 select_reduce_fusion.3
  9.6 1.5 fusion.94
  15.8 15.3 %broadcast_multiply_fusion = f32[6,512,6,256]{3,1,2,0:T(8,128)} fusion(f32[6,512,6,256]{3,1,2,0:T(8,128)} %param.17, f32[6,512,6]{1,2,0:T(8,128)S(1)} %multiply_bitcast_fusion.10), kind=kLoop, calls=%fused_computation.18 | loop fusion | flops 4718592 | bytes 37822464 | tf_op jit(solution)/shard_map/mul | solution.py:36
  31.1 10.7 fusion.93
  41.9 1.1 pad_maximum_fusion
  43.1 8.5 all_gather.18
  53.4 10.7 broadcast_select_fusion
  64.1 8.5 copy-done
  72.5 3.9 fusion.76
  76.5 1.2 fusion.59
  77.7 0.9 slice_bitcast_fusion.40
  78.6 92.2 %all-gather.6.cloned.1.call-done = f32[2,512,2048]{2,1,0:T(8,128)} async-done(((f32[2,512,256]{2,1,0:T(8,128)}), f32[2,512,2048]{2,1,0:T(8,128)}) %all-gather.6.cloned.1.call-update) | async-done | bytes 8388624 | tf_op jit(solution)/shard_map/all_gather | solution.py:67
  170.8 11.2 convolution_bitcast_fusion.4
  186.9 2.5 multiply_bitcast_fusion.5
  189.3 1.0 pad_maximum_fusion.1
  190.5 9.0 scatter.20
  199.4 33.4 %all-reduce.7.cloned.1.call-done = f32[2048,264]{0,1:T(8,128)} async-done(((f32[2048,264]{0,1:T(8,128)}), f32[2048,264]{0,1:T(8,128)}) %all-reduce.7.cloned.1.call-update) | async-done | bytes 2162704 | tf_op jit(solution)/shard_map/psum | solution.py:68
  232.8 0.8 slice_subtract_fusion.4
  233.7 1.8 slice_negate_fusion.4
  235.5 9.8 fusion.73
  245.3 3.7 dynamic-slice_bitcast_fusion.7
  249.0 1.1 slice_bitcast_fusion.38
  250.1 1.1 slice_bitcast_fusion.39
  251.2 108.7 %all-gather.8.cloned.1.call-done = f32[2,512,2048]{2,1,0:T(8,128)} async-done(((f32[2,512,256]{2,1,0:T(8,128)}), f32[2,512,2048]{2,1,0:T(8,128)}) %all-gather.8.cloned.1.call-update) | async-done | bytes 8388624 | tf_op jit(solution)/shard_map/all_gather | solution.py:67
  359.9 18.0 %convolution_bitcast_fusion.3 = f32[2048,520]{0,1:T(8,128)} fusion(f32[2,512,2048]{2,1,0:T(8,128)} %all-gather.8.cloned.1.call-done, f32[1,512,520]{1,2,0:T(8,128)} %slice_bitcast_fusion.38, f32[1,512,520]{1,2,0:T(8,128)} %slice_bitcast_fusion.39), kind=kOutput, calls=%fused_computation.57 | convolution fusion | flops 13086760960 | bytes 14778368 | tf_op jit(solution)/shard_map/tiw,tin->wn/dot_general | solution.py:11
  378.0 1.0 copy-done.1
  379.0 1.0 pad_maximum_fusion.2
  380.1 82.8 %all-reduce.9.cloned.1.call-done = f32[2048,520]{0,1:T(8,128)} async-done(((f32[2048,520]{0,1:T(8,128)}), f32[2048,520]{0,1:T(8,128)}) %all-reduce.9.cloned.1.call-update) | async-done | bytes 4259856 | tf_op jit(solution)/shard_map/psum | solution.py:68
  462.9 0.8 slice_subtract_fusion.3
  463.7 2.5 slice_negate_fusion.3
  466.3 13.2 bitcast_dynamic-update-slice_fusion
  479.5 3.6 dynamic-slice_bitcast_fusion.5
  483.1 1.3 slice_bitcast_fusion.28
  484.4 1.3 slice_bitcast_fusion.29
  485.7 104.2 %all-gather.10.cloned.1.call-done = f32[2,512,2048]{2,1,0:T(8,128)} async-done(((f32[2,512,256]{2,1,0:T(8,128)}), f32[2,512,2048]{2,1,0:T(8,128)}) %all-gather.10.cloned.1.call-update) | async-done | bytes 8388624 | tf_op jit(solution)/shard_map/all_gather | solution.py:67
  589.9 25.4 %convolution_bitcast_fusion.2 = f32[2048,776]{0,1:T(8,128)} fusion(f32[2,512,2048]{2,1,0:T(8,128)} %all-gather.10.cloned.1.call-done, f32[1,512,776]{1,2,0:T(8,128)} %slice_bitcast_fusion.28, f32[1,512,776]{1,2,0:T(8,128)} %slice_bitcast_fusion.29), kind=kOutput, calls=%fused_computation.56 | convolution fusion | flops 19529474048 | bytes 17924096 | tf_op jit(solution)/shard_map/tiw,tin->wn/dot_general | solution.py:11
  620.4 1.7 multiply_bitcast_fusion.1
  622.1 1.1 pad_maximum_fusion.3
  623.3 111.1 %all-reduce.11.cloned.1.call-done = f32[2048,776]{0,1:T(8,128)} async-done(((f32[2048,776]{0,1:T(8,128)}), f32[2048,776]{0,1:T(8,128)}) %all-reduce.11.cloned.1.call-update) | async-done | bytes 6357008 | tf_op jit(solution)/shard_map/psum | solution.py:68
  734.3 0.8 slice_subtract_fusion.2
  735.2 3.4 slice_negate_fusion.2
  738.6 17.0 %fusion.53 = f32[6,512,1544]{1,2,0:T(8,128)} fusion(f32[6,512,1544]{1,2,0:T(8,128)} %bitcast_dynamic-update-slice_fusion, f32[2048,8]{0,1:T(8,128)S(1)} %slice_subtract_fusion.2, f32[2048,768]{0,1:T(8,128)S(1)} %slice_negate_fusion.2, f32[2048,256]{0,1:T(8,128)S(1)} %fusion.67, f32[6,2048,512]{2,1,0:T(8,128)} %copy-done), kind=kOutput, calls=%fused_computation.63 | convolution fusion | flops 12989792256 | bytes 14761984 | tf_op jit(solution)/shard_map/dot_general | solution.py:74
  755.5 3.6 dynamic-slice_bitcast_fusion.3
  759.1 1.5 slice_bitcast_fusion.26
  760.6 1.5 slice_bitcast_fusion.27
  762.1 99.4 %all-gather.12.cloned.1.call-done = f32[2,512,2048]{2,1,0:T(8,128)} async-done(((f32[2,512,256]{2,1,0:T(8,128)}), f32[2,512,2048]{2,1,0:T(8,128)}) %all-gather.12.cloned.1.call-update) | async-done | bytes 8388624 | tf_op jit(solution)/shard_map/all_gather | solution.py:67
  861.5 31.5 %convolution_bitcast_fusion.1 = f32[2048,1032]{0,1:T(8,128)} fusion(f32[2,512,2048]{2,1,0:T(8,128)} %all-gather.12.cloned.1.call-done, f32[1,512,1032]{1,2,0:T(8,128)} %slice_bitcast_fusion.26, f32[1,512,1032]{1,2,0:T(8,128)} %slice_bitcast_fusion.27), kind=kOutput, calls=%fused_computation.20 | convolution fusion | flops 25972187136 | bytes 21069824 | tf_op jit(solution)/shard_map/tiw,tin->wn/dot_general | solution.py:11
  893.1 1.0 pad_maximum_fusion.4
  894.4 150.9 %all-reduce.13.cloned.1.call-done = f32[2048,1032]{0,1:T(8,128)} async-done(((f32[2048,1032]{0,1:T(8,128)}), f32[2048,1032]{0,1:T(8,128)}) %all-reduce.13.cloned.1.call-update) | async-done | bytes 8454160 | tf_op jit(solution)/shard_map/psum | solution.py:68
  1045.3 0.8 slice_subtract_fusion.1
  1046.2 4.3 slice_negate_fusion.1
  1050.4 20.4 %fusion.41 = f32[6,512,1544]{1,2,0:T(8,128)} fusion(f32[6,512,1544]{1,2,0:T(8,128)} %fusion.53, f32[2048,8]{0,1:T(8,128)S(1)} %slice_subtract_fusion.1, f32[2048,1024]{0,1:T(8,128)S(1)} %slice_negate_fusion.1, f32[2048,256]{0,1:T(8,128)S(1)} %fusion.67, f32[6,2048,512]{2,1,0:T(8,128)} %copy-done), kind=kOutput, calls=%fused_computation.59 | convolution fusion | flops 16212066304 | bytes 17383424 | tf_op jit(solution)/shard_map/dot_general | solution.py:74
  1070.8 3.6 dynamic-slice_bitcast_fusion.1
  1074.5 1.7 slice_bitcast_fusion.24
  1076.2 1.7 slice_bitcast_fusion.25
  1077.9 94.5 %all-gather.14.cloned.1.call-done = f32[2,512,2048]{2,1,0:T(8,128)} async-done(((f32[2,512,256]{2,1,0:T(8,128)}), f32[2,512,2048]{2,1,0:T(8,128)}) %all-gather.14.cloned.1.call-update) | async-done | bytes 8388624 | tf_op jit(solution)/shard_map/all_gather | solution.py:67
  1172.5 42.1 %convolution_bitcast_fusion = f32[2048,1288]{0,1:T(8,128)} fusion(f32[2,512,2048]{2,1,0:T(8,128)} %all-gather.14.cloned.1.call-done, f32[1,512,1288]{1,2,0:T(8,128)} %slice_bitcast_fusion.24, f32[1,512,1288]{1,2,0:T(8,128)} %slice_bitcast_fusion.25), kind=kOutput, calls=%fused_computation.19 | convolution fusion | flops 32414900224 | bytes 24215552 | tf_op jit(solution)/shard_map/tiw,tin->wn/dot_general | solution.py:11
  1214.6 186.2 %all-reduce.15.cloned.1.call-done = f32[2048,1288]{0,1:T(8,128)} async-done(((f32[2048,1288]{0,1:T(8,128)}), f32[2048,1288]{0,1:T(8,128)}) %all-reduce.15.cloned.1.call-update) | async-done | bytes 10551312 | tf_op jit(solution)/shard_map/psum | solution.py:68
  1400.7 5.1 slice_negate_fusion
  1405.8 0.8 slice_subtract_fusion
  1406.7 23.9 %fusion.47 = f32[6,512,1544]{1,2,0:T(8,128)} fusion(f32[6,512,1544]{1,2,0:T(8,128)} %fusion.41, f32[2048,8]{0,1:T(8,128)S(1)} %slice_subtract_fusion, f32[2048,1280]{0,1:T(8,128)S(1)} %slice_negate_fusion, f32[2048,256]{0,1:T(8,128)S(1)} %fusion.67, f32[6,2048,512]{2,1,0:T(8,128)} %copy-done), kind=kOutput, calls=%fused_computation.61 | convolution fusion | flops 19434340352 | bytes 20004864 | tf_op jit(solution)/shard_map/dot_general | solution.py:74
  1430.6 1.5 slice.382
  1432.1 8.8 fusion
  1440.9 37.7 %psum.47 = f32[6,512]{1,0:T(8,128)} all-reduce(f32[6,512]{1,0:T(8,128)S(1)} %fusion), channel_id=1, replica_groups=mesh['row'=4,'col'=8] {'col'}, use_global_device_ids=true, to_apply=%region_10.11 | all-reduce | flops 3072 | bytes 24576 | tf_op jit(solution)/shard_map/psum | solution.py:81
  (45 shorter events, 6.4 us)
Async XLA Ops:
  7.2 163.6 %all-gather.6.cloned.1.call-start = ((), (), s32[]{:S(2)}) async-start(), calls=%async_computation | async-start | bytes 9437184 | tf_op jit(solution)/shard_map/all_gather | solution.py:67
  41.8 1.3 copy-start.4
  43.0 189.8 %all-reduce.7.cloned.1.call-start = ((), (), s32[]{:S(2)}) async-start(), calls=%async_computation.1 | async-start | bytes 4325376 | tf_op jit(solution)/shard_map/psum | solution.py:68
  51.6 0.8 copy-start.2
  64.1 8.5 copy-start
  182.0 177.9 %all-gather.8.cloned.1.call-start = ((), (), s32[]{:S(2)}) async-start(), calls=%async_computation.2 | async-start | bytes 9437184 | tf_op jit(solution)/shard_map/all_gather | solution.py:67
  190.4 42.4 %copy-start.3 = (f32[6,2048,8]{1,2,0:T(8,128)S(1)}, f32[6,2048,8]{1,2,0:T(8,128)}, u32[]{:S(2)}) copy-start(f32[6,2048,8]{1,2,0:T(8,128)} %copy-done.2) | copy-start | bytes 1179652
  190.4 272.5 %all-reduce.9.cloned.1.call-start = ((), (), s32[]{:S(2)}) async-start(), calls=%async_computation.3 | async-start | bytes 8519680 | tf_op jit(solution)/shard_map/psum | solution.py:68
  378.0 1.0 copy-start.1
  378.0 211.9 %all-gather.10.cloned.1.call-start = ((), (), s32[]{:S(2)}) async-start(), calls=%async_computation.4 | async-start | bytes 9437184 | tf_op jit(solution)/shard_map/all_gather | solution.py:67
  380.0 354.3 %all-reduce.11.cloned.1.call-start = ((), (), s32[]{:S(2)}) async-start(), calls=%async_computation.5 | async-start | bytes 12713984 | tf_op jit(solution)/shard_map/psum | solution.py:68
  615.3 246.2 %all-gather.12.cloned.1.call-start = ((), (), s32[]{:S(2)}) async-start(), calls=%async_computation.6 | async-start | bytes 9437184 | tf_op jit(solution)/shard_map/all_gather | solution.py:67
  623.2 422.1 %all-reduce.13.cloned.1.call-start = ((), (), s32[]{:S(2)}) async-start(), calls=%async_computation.7 | async-start | bytes 16908288 | tf_op jit(solution)/shard_map/psum | solution.py:68
  893.0 279.4 %all-gather.14.cloned.1.call-start = ((), (), s32[]{:S(2)}) async-start(), calls=%async_computation.8 | async-start | bytes 9437184 | tf_op jit(solution)/shard_map/all_gather | solution.py:67
  894.2 506.6 %all-reduce.15.cloned.1.call-start = ((), (), s32[]{:S(2)}) async-start(), calls=%async_computation.9 | async-start | bytes 21102592 | tf_op jit(solution)/shard_map/psum | solution.py:68
Sparse Core Ops, SparseCore 0:
  43.1 127.6 all-gather.5
  182.1 50.6 all-reduce.6
  234.9 124.9 all-gather.7
  378.1 84.7 all-reduce.8
  464.8 125.0 all-gather.9
  615.5 118.8 all-reduce.10
  736.4 125.1 all-gather.11
  893.2 152.0 all-reduce.12
  1047.4 125.0 all-gather.13
  1214.7 185.9 all-reduce.14
where the time goes:
time: 1490 us
  waiting for transfers between devices  1060 us (71%)
  matrix products  216 us (14%)
  other arithmetic  70.2 us (5%)
  local copies, waits for them, and re-layouts  61.6 us (4%)
  blocking collectives  46.2 us (3%)
  between operations  27.1 us (2%)
    psum x5, waiting for transfers between devices, body(): summed = lax.psum(partial_value, 'row')  564 us
    all_gather x5, waiting for transfers between devices, body(): lax.all_gather(blocks, 'col', axis=2, tiled=True)  499 us
    dot_general x5, matrix products, contract(): return jnp.einsum('tiw,tin->wn', panel_piece, selected, precision=HIGHEST)  128 us
    dot_general x6, matrix products, body(): jnp.dot(lower_inv[current_sup].T, right, precision=HIGHEST, preferred_ele...  88.2 us
    psum x1, blocking collectives, body(): variance = lax.psum(squares, 'col')  37.7 us
  transfers between devices with their start and end apart: 10, of which 10 were waited for; matrix products, arithmetic and copies ran while one was open for 9% of the time, Pallas kernels for 0%

commit v1 on v0

--- a/solution.py
+++ b/solution.py
@@ -65,7 +65,11 @@
             blocks = jnp.stack(picks)
             selected = jnp.stack(chosen_rows)
             partial_value = contract(selected, lax.all_gather(blocks, "col", axis=2, tiled=True))
-            summed = lax.psum(partial_value, "row")
+            size = lax.axis_size("row")
+            summed, hop = (partial_value, 1)
+            while hop < size:
+                summed = summed + lax.ppermute(summed, "row", [(i, i ^ hop) for i in range(size)])
+                hop = 2 * hop
         split_at = summed.shape[1] - rhs_width
         remaining = jnp.concatenate(
             [-summed[:, :split_at], gathered[current_sup] - summed[:, split_at:]], axis=1

time: 1490 us -> 1310 us (0.88)
  waiting for transfers between devices: 1060 us -> 851 us
  other arithmetic: 70.2 us -> 109 us
    ppermute x0 -> x10, waiting for transfers between devices: none -> 721 us  [body(): lax.ppermute(summed, 'row', [(i, i ^ hop) for i in range(size)])]
    psum x5 -> x0, waiting for transfers between devices: 564 us -> none  [body(): summed = lax.psum(partial_value, 'row')]
    all_gather x5, waiting for transfers between devices: 499 us -> 131 us  [body(): lax.all_gather(blocks, 'col', axis=2, tiled=True)]
    add x0 -> x10, other arithmetic: none -> 47.2 us  [body(): summed + lax.ppermute(summed, 'row', [(i, i ^ hop) for i in range(size)])]
  transfers between devices with their start and end apart: 10 -> 15, of which waited for: 10 -> 12; matrix products, arithmetic and copies ran while one was open for 9% -> 15% of each run, Pallas kernels for 0% -> 0%
where the time goes in v1:
time: 1310 us
  waiting for transfers between devices  851 us (65%)
  matrix products  211 us (16%)
  other arithmetic  109 us (8%)
  local copies, waits for them, and re-layouts  58 us (4%)
  blocking collectives  43.2 us (3%)
  between operations  27.4 us (2%)
    ppermute x10, waiting for transfers between devices, body(): lax.ppermute(summed, 'row', [(i, i ^ hop) for i in range(size)])  721 us
    all_gather x5, waiting for transfers between devices, body(): lax.all_gather(blocks, 'col', axis=2, tiled=True)  131 us
    dot_general x5, matrix products, contract(): return jnp.einsum('tiw,tin->wn', panel_piece, selected, precision=HIGHEST)  123 us
    dot_general x6, matrix products, body(): jnp.dot(lower_inv[current_sup].T, right, precision=HIGHEST, preferred_ele...  88.6 us
    add x10, other arithmetic, body(): summed + lax.ppermute(summed, 'row', [(i, i ^ hop) for i in range(size)])  47.2 us
    psum x1, blocking collectives, body(): variance = lax.psum(squares, 'col')  34.8 us
  transfers between devices with their start and end apart: 15, of which 12 were waited for; matrix products, arithmetic and copies ran while one was open for 15% of the time, Pallas kernels for 0%

profile of v1, /device:TPU:0, one launch (start us, length us, event | category | flops | bytes accessed | tf_op | source)
XLA Modules:
  0.0 1308.9 jit_solution(8952671878666658900)
XLA Ops:
  9.6 1.5 fusion.94
  16.0 15.3 %broadcast_multiply_fusion = f32[6,512,6,256]{3,1,2,0:T(8,128)} fusion(f32[6,512,6,256]{3,1,2,0:T(8,128)} %param.17, f32[6,512,6]{1,2,0:T(8,128)S(1)} %multiply_bitcast_fusion.10), kind=kLoop, calls=%fused_computation.18 | loop fusion | flops 4718592 | bytes 37822464 | tf_op jit(solution)/shard_map/mul | solution.py:36
  31.3 10.8 fusion.93
  42.0 1.3 multiply_bitcast_fusion.9
  49.6 2.3 multiply_bitcast_fusion.5
  53.0 8.3 all_gather.18
  62.4 10.9 broadcast_select_fusion
  73.4 8.4 copy-done
  81.8 4.0 fusion.76
  85.8 1.2 fusion.59
  87.1 85.1 %all-gather.6.cloned.1.call-done = f32[2,512,2048]{2,1,0:T(8,128)} async-done(((f32[2,512,256]{2,1,0:T(8,128)}), f32[2,512,2048]{2,1,0:T(8,128)}) %all-gather.6.cloned.1.call-update) | async-done | bytes 8388624 | tf_op jit(solution)/shard_map/all_gather | solution.py:67
  172.2 10.0 convolution_bitcast_fusion.4
  182.4 4.2 collective-permute-done
  187.0 1.6 collective-permute-start.1
  189.9 8.9 scatter.20
  198.8 37.4 %collective-permute-done.1 = f32[2048,264]{0,1:T(8,128)} collective-permute-done((f32[2048,264]{0,1:T(8,128)S(1)}, f32[2048,264]{0,1:T(8,128)}, u32[]{:S(2)}, u32[]{:S(2)}) %collective-permute-start.1) | collective-permute-done | bytes 2162720 | tf_op jit(solution)/shard_map/ppermute | solution.py:71
  236.2 1.9 add.147
  238.4 9.6 fusion.73
  248.0 3.6 dynamic-slice_bitcast_fusion.7
  251.7 45.7 %all-gather.8.cloned.1.call-done = f32[2,512,2048]{2,1,0:T(8,128)} async-done(((f32[2,512,256]{2,1,0:T(8,128)}), f32[2,512,2048]{2,1,0:T(8,128)}) %all-gather.8.cloned.1.call-update) | async-done | bytes 8388624 | tf_op jit(solution)/shard_map/all_gather | solution.py:67
  297.4 16.5 %convolution_bitcast_fusion.3 = f32[2048,520]{0,1:T(8,128)S(1)} fusion(f32[2,512,2048]{2,1,0:T(8,128)} %all-gather.8.cloned.1.call-done, f32[1,512,520]{1,2,0:T(8,128)S(1)} %slice_bitcast_fusion.38, f32[1,512,520]{1,2,0:T(8,128)S(1)} %slice_bitcast_fusion.39), kind=kOutput, calls=%fused_computation.57 | convolution fusion | flops 13086760960 | bytes 14778368 | tf_op jit(solution)/shard_map/tiw,tin->wn/dot_general | solution.py:11
  314.0 7.2 collective-permute-done.2
  321.2 1.1 add.150
  322.3 1.6 collective-permute-start.3
  323.9 92.5 %collective-permute-done.3 = f32[2048,520]{0,1:T(8,128)S(1)} collective-permute-done((f32[2048,520]{0,1:T(8,128)S(1)}, f32[2048,520]{0,1:T(8,128)S(1)}, u32[]{:S(2)}, u32[]{:S(2)}) %collective-permute-start.3) | collective-permute-done | bytes 4259872 | tf_op jit(solution)/shard_map/ppermute | solution.py:71
  417.9 1.2 copy-done.3
  419.1 12.8 bitcast_dynamic-update-slice_fusion
  431.9 3.6 dynamic-slice_bitcast_fusion.5
  435.5 1.3 slice_bitcast_fusion.28
  436.8 1.3 slice_bitcast_fusion.29
  438.1 25.7 %convolution_bitcast_fusion.2 = f32[2048,776]{0,1:T(8,128)} fusion(f32[2,512,2048]{2,1,0:T(8,128)} %all-gather.10.cloned.1.call-done, f32[1,512,776]{1,2,0:T(8,128)} %slice_bitcast_fusion.28, f32[1,512,776]{1,2,0:T(8,128)} %slice_bitcast_fusion.29), kind=kOutput, calls=%fused_computation.56 | convolution fusion | flops 19529474048 | bytes 17924096 | tf_op jit(solution)/shard_map/tiw,tin->wn/dot_general | solution.py:11
  469.0 1.7 multiply_bitcast_fusion.1
  471.7 2.6 collective-permute-done.4
  474.3 6.7 add.154
  481.0 1.5 collective-permute-start.5
  482.5 137.6 %collective-permute-done.5 = f32[2048,776]{0,1:T(8,128)} collective-permute-done((f32[2048,776]{0,1:T(8,128)S(1)}, f32[2048,776]{0,1:T(8,128)}, u32[]{:S(2)}, u32[]{:S(2)}) %collective-permute-start.5) | collective-permute-done | bytes 6357024 | tf_op jit(solution)/shard_map/ppermute | solution.py:71
  620.1 4.1 add.155
  624.2 1.1 slice_negate_fusion.2
  625.4 17.0 %fusion.53 = f32[6,512,1544]{1,2,0:T(8,128)} fusion(f32[6,512,1544]{1,2,0:T(8,128)} %bitcast_dynamic-update-slice_fusion, f32[2048,8]{0,1:T(8,128)S(1)} %slice_subtract_fusion.2, f32[2048,768]{0,1:T(8,128)S(1)} %slice_negate_fusion.2, f32[2048,256]{0,1:T(8,128)S(1)} %copy-done.3, f32[6,2048,512]{2,1,0:T(8,128)} %copy-done), kind=kOutput, calls=%fused_computation.63 | convolution fusion | flops 12989792256 | bytes 14761984 | tf_op jit(solution)/shard_map/dot_general | solution.py:78
  642.4 3.6 dynamic-slice_bitcast_fusion.3
  645.9 1.5 slice_bitcast_fusion.26
  647.5 1.5 slice_bitcast_fusion.27
  648.9 31.9 %convolution_bitcast_fusion.1 = f32[2048,1032]{0,1:T(8,128)} fusion(f32[2,512,2048]{2,1,0:T(8,128)} %all-gather.12.cloned.1.call-done, f32[1,512,1032]{1,2,0:T(8,128)} %slice_bitcast_fusion.26, f32[1,512,1032]{1,2,0:T(8,128)} %slice_bitcast_fusion.27), kind=kOutput, calls=%fused_computation.20 | convolution fusion | flops 25972187136 | bytes 21069824 | tf_op jit(solution)/shard_map/tiw,tin->wn/dot_general | solution.py:11
  681.9 12.5 collective-permute-done.6
  694.5 12.1 add.158
  706.6 1.5 collective-permute-start.7
  708.1 182.7 %collective-permute-done.7 = f32[2048,1032]{0,1:T(8,128)} collective-permute-done((f32[2048,1032]{0,1:T(8,128)}, f32[2048,1032]{0,1:T(8,128)}, u32[]{:S(2)}, u32[]{:S(2)}) %collective-permute-start.7) | collective-permute-done | bytes 8454176 | tf_op jit(solution)/shard_map/ppermute | solution.py:71
  890.8 12.1 add.159
  903.7 4.3 slice_negate_fusion.1
  908.0 20.4 %fusion.41 = f32[6,512,1544]{1,2,0:T(8,128)} fusion(f32[6,512,1544]{1,2,0:T(8,128)} %fusion.53, f32[2048,8]{0,1:T(8,128)S(1)} %slice_subtract_fusion.1, f32[2048,1024]{0,1:T(8,128)S(1)} %slice_negate_fusion.1, f32[2048,256]{0,1:T(8,128)S(1)} %copy-done.3, f32[6,2048,512]{2,1,0:T(8,128)} %copy-done), kind=kOutput, calls=%fused_computation.59 | convolution fusion | flops 16212066304 | bytes 17383424 | tf_op jit(solution)/shard_map/dot_general | solution.py:78
  928.4 3.6 dynamic-slice_bitcast_fusion.1
  932.0 1.8 slice_bitcast_fusion.24
  933.8 1.7 slice_bitcast_fusion.25
  935.5 38.5 %convolution_bitcast_fusion = f32[2048,1288]{0,1:T(8,128)S(1)} fusion(f32[2,512,2048]{2,1,0:T(8,128)} %all-gather.14.cloned.1.call-done, f32[1,512,1288]{1,2,0:T(8,128)} %slice_bitcast_fusion.24, f32[1,512,1288]{1,2,0:T(8,128)} %slice_bitcast_fusion.25), kind=kOutput, calls=%fused_computation.19 | convolution fusion | flops 32414900224 | bytes 24215552 | tf_op jit(solution)/shard_map/tiw,tin->wn/dot_general | solution.py:11
  974.1 16.2 %collective-permute-done.8 = f32[2048,1288]{0,1:T(8,128)S(1)} collective-permute-done((f32[2048,1288]{0,1:T(8,128)S(1)}, f32[2048,1288]{0,1:T(8,128)S(1)}, u32[]{:S(2)}, u32[]{:S(2)}) %collective-permute-start.8) | collective-permute-done | bytes 10551328 | tf_op jit(solution)/shard_map/ppermute | solution.py:71
  990.3 2.5 add.162
  992.8 1.6 collective-permute-start.9
  994.4 227.5 %collective-permute-done.9 = f32[2048,1288]{0,1:T(8,128)} collective-permute-done((f32[2048,1288]{0,1:T(8,128)S(1)}, f32[2048,1288]{0,1:T(8,128)}, u32[]{:S(2)}, u32[]{:S(2)}) %collective-permute-start.9) | collective-permute-done | bytes 10551328 | tf_op jit(solution)/shard_map/ppermute | solution.py:71
  1221.8 5.3 add.163
  1227.2 5.1 slice_negate_fusion
  1232.3 24.7 %fusion.47 = f32[6,512,1544]{1,2,0:T(8,128)} fusion(f32[6,512,1544]{1,2,0:T(8,128)} %fusion.41, f32[2048,8]{0,1:T(8,128)S(1)} %slice_subtract_fusion, f32[2048,1280]{0,1:T(8,128)} %slice_negate_fusion, f32[2048,256]{0,1:T(8,128)S(1)} %copy-done.3, f32[6,2048,512]{2,1,0:T(8,128)} %copy-done), kind=kOutput, calls=%fused_computation.61 | convolution fusion | flops 19434340352 | bytes 20004864 | tf_op jit(solution)/shard_map/dot_general | solution.py:78
  1257.0 1.5 slice.382
  1258.5 8.8 fusion
  1267.3 34.8 %psum.7 = f32[6,512]{1,0:T(8,128)} all-reduce(f32[6,512]{1,0:T(8,128)S(1)} %fusion), channel_id=1, replica_groups=mesh['row'=4,'col'=8] {'col'}, use_global_device_ids=true, to_apply=%region_5.6 | all-reduce | flops 3072 | bytes 24576 | tf_op jit(solution)/shard_map/psum | solution.py:85
  (62 shorter events, 14.7 us)
Async XLA Ops:
  7.2 165.1 %all-gather.6.cloned.1.call-start = ((), (), s32[]{:S(2)}) async-start(), calls=%async_computation | async-start | bytes 9437184 | tf_op jit(solution)/shard_map/all_gather | solution.py:67
  44.4 253.0 %all-gather.8.cloned.1.call-start = ((), (), s32[]{:S(2)}) async-start(), calls=%async_computation.1 | async-start | bytes 9437184 | tf_op jit(solution)/shard_map/all_gather | solution.py:67
  52.9 385.1 %all-gather.10.cloned.1.call-start = ((), (), s32[]{:S(2)}) async-start(), calls=%async_computation.2 | async-start | bytes 9437184 | tf_op jit(solution)/shard_map/all_gather | solution.py:67
  62.4 11.0 copy-start.1
  73.4 8.4 copy-start
  182.3 6.3 copy-start.4
  182.3 6.3 copy-start.5
  182.3 4.3 collective-permute-start
  187.0 49.2 %collective-permute-start.1 = (f32[2048,264]{0,1:T(8,128)S(1)}, f32[2048,264]{0,1:T(8,128)}, u32[]{:S(2)}, u32[]{:S(2)}) collective-permute-start(f32[2048,264]{0,1:T(8,128)S(1)} %add.146), channel_id=1, source_target_pairs={{0,16},{8,24},{16,0},{24,8},{1,17},{9,25},{17,1},{25,9},{2,18},{10... | collective-permute-start | bytes 6488072 | tf_op jit(solution)/shard_map/ppermute | solution.py:71
  189.7 459.3 %all-gather.12.cloned.1.call-start = ((), (), s32[]{:S(2)}) async-start(), calls=%async_computation.3 | async-start | bytes 9437184 | tf_op jit(solution)/shard_map/all_gather | solution.py:67
  198.8 39.5 %copy-start.2 = (f32[2048,256]{0,1:T(8,128)S(1)}, f32[2048,256]{0,1:T(8,128)}, u32[]{:S(2)}) copy-start(f32[2048,256]{0,1:T(8,128)} %copy-done.1) | copy-start | bytes 6291460
  313.9 7.3 collective-permute-start.2
  322.3 94.1 %collective-permute-start.3 = (f32[2048,520]{0,1:T(8,128)S(1)}, f32[2048,520]{0,1:T(8,128)S(1)}, u32[]{:S(2)}, u32[]{:S(2)}) collective-permute-start(f32[2048,520]{0,1:T(8,128)S(1)} %add.150), channel_id=1, source_target_pairs={{0,16},{8,24},{16,0},{24,8},{1,17},{9,25},{17,1},{25,9},{2,18},{10... | collective-permute-start | bytes 12779528 | tf_op jit(solution)/shard_map/ppermute | solution.py:71
  417.5 1.6 copy-start.3
  463.7 10.6 collective-permute-start.4
  471.7 463.8 %all-gather.14.cloned.1.call-start = ((), (), s32[]{:S(2)}) async-start(), calls=%async_computation.4 | async-start | bytes 9437184 | tf_op jit(solution)/shard_map/all_gather | solution.py:67
  481.0 139.1 %collective-permute-start.5 = (f32[2048,776]{0,1:T(8,128)S(1)}, f32[2048,776]{0,1:T(8,128)}, u32[]{:S(2)}, u32[]{:S(2)}) collective-permute-start(f32[2048,776]{0,1:T(8,128)S(1)} %add.154), channel_id=1, source_target_pairs={{0,16},{8,24},{16,0},{24,8},{1,17},{9,25},{17,1},{25,9},{2,18},{10... | collective-permute-start | bytes 19070984 | tf_op jit(solution)/shard_map/ppermute | solution.py:71
  680.8 13.7 %collective-permute-start.6 = (f32[2048,1032]{0,1:T(8,128)}, f32[2048,1032]{0,1:T(8,128)}, u32[]{:S(2)}, u32[]{:S(2)}) collective-permute-start(f32[2048,1032]{0,1:T(8,128)} %convolution_bitcast_fusion.1), channel_id=1, source_target_pairs={{0,8},{8,0},{16,24},{24,16},{1,9},{9,1},{17,25},{25,17},{2,10},{10... | collective-permute-start | bytes 25362440 | tf_op jit(solution)/shard_map/ppermute | solution.py:71
  706.6 184.2 %collective-permute-start.7 = (f32[2048,1032]{0,1:T(8,128)}, f32[2048,1032]{0,1:T(8,128)}, u32[]{:S(2)}, u32[]{:S(2)}) collective-permute-start(f32[2048,1032]{0,1:T(8,128)} %add.158), channel_id=1, source_target_pairs={{0,16},{8,24},{16,0},{24,8},{1,17},{9,25},{17,1},{25,9},{2,18},{10... | collective-permute-start | bytes 25362440 | tf_op jit(solution)/shard_map/ppermute | solution.py:71
  974.0 16.3 %collective-permute-start.8 = (f32[2048,1288]{0,1:T(8,128)S(1)}, f32[2048,1288]{0,1:T(8,128)S(1)}, u32[]{:S(2)}, u32[]{:S(2)}) collective-permute-start(f32[2048,1288]{0,1:T(8,128)S(1)} %convolution_bitcast_fusion), channel_id=1, source_target_pairs={{0,8},{8,0},{16,24},{24,16},{1,9},{9,1},{17,25},{25,17},{2,10},{10... | collective-permute-start | bytes 31653896 | tf_op jit(solution)/shard_map/ppermute | solution.py:71
  992.8 229.0 %collective-permute-start.9 = (f32[2048,1288]{0,1:T(8,128)S(1)}, f32[2048,1288]{0,1:T(8,128)}, u32[]{:S(2)}, u32[]{:S(2)}) collective-permute-start(f32[2048,1288]{0,1:T(8,128)S(1)} %add.162), channel_id=1, source_target_pairs={{0,16},{8,24},{16,0},{24,8},{1,17},{9,25},{17,1},{25,9},{2,18},{10... | collective-permute-start | bytes 31653896 | tf_op jit(solution)/shard_map/ppermute | solution.py:71
Sparse Core Ops, SparseCore 0:
  44.5 127.6 all-gather.5
  174.3 123.1 all-gather.7
  299.5 123.1 all-gather.9
  471.8 123.2 all-gather.11
  682.0 123.1 all-gather.13
